TPU v7x, 512 devices: a whole 4x4x16 slice. The times are simulated.
512 devices in a mesh: rep: 4 (over x), rows: 128 (over y, z, core).
Axes of the slice: x: 4, y: 4, z: 16, core: 2. Of those that a mesh axis runs over, the one named last changes fastest.
Arguments:
- features: bfloat16 [65536, 256], P('rows'), may hold values from -6 to 6
- tiles: bfloat16 [128, 4, 2, 256, 256], P('rows', 'rep'), may hold values from -0.1875 to 0.1875
- tile_row: int32 [128, 4, 2], P('rows', 'rep'), may hold values from 0 to 1, as said below
- tile_col: int32 [128, 4, 2], P('rows', 'rep'), may hold values from 0 to 3, as said below
- tile_live: int32 [128, 4], P('rows', 'rep'), may hold values from 1 to 2, as said below
- send_index: int32 [128, 128, 4], P('rows'), may hold values from 0 to 511
- gain: float32 [3, 256], replicated, may hold values from 0.1 to 1.9
- w_in: bfloat16 [3, 256, 512], replicated, may hold values from -0.375 to 0.375
- w_out: bfloat16 [3, 512, 256], replicated, may hold values from -0.25 to 0.25
Outputs:
- result: bfloat16 [65536, 256], P('rows')
Inputs may be any that keep to these rules, and one draw needn't show every extreme that they name: `tile_live`: every owner and section has at least one slot in use, and some owner and section has all 2. For each owner, the pairs (tile_row, tile_col) over all sections and slots are all different. For each owner, the pairs (tile_row, tile_col) over all sections and slots are all different.
All inputs are finite; a program needn't handle non-finite values.
Results may differ from a plain program's by a relative error of at most 0.012.
Values may be sent and summed in bfloat16 or wider, within the bound.
A program may use at most 64 MiB of HBM per device.

v0:
```python
import jax
import jax.numpy as jnp
from jax import lax
from jax.sharding import PartitionSpec as P

HOPS = 3


def update_rows(current_rows, gathered, gain_row, first, second):
    mixed = current_rows.astype(jnp.float32) + gathered
    scale = lax.rsqrt(jnp.mean(mixed * mixed, axis=-1, keepdims=True) + 1e-06)
    normed = (mixed * scale * gain_row[None, :]).astype(jnp.bfloat16)
    inner = jax.nn.gelu(jnp.dot(normed, first, preferred_element_type=jnp.float32)).astype(
        jnp.bfloat16
    )
    return (mixed + jnp.dot(inner, second, preferred_element_type=jnp.float32)).astype(jnp.bfloat16)


def per_device(features, tiles, tile_row, tile_col, tile_live, send_index, gain, w_in, w_out):
    owners = lax.axis_size("rows")
    nodes = features.shape[0]
    width = features.shape[1]
    tile_side = tiles.shape[-1]
    slots = tiles.shape[2]
    halo_width = send_index.shape[2]
    halo_pad = (owners * halo_width + tile_side - 1) // tile_side * tile_side
    row_tiles = nodes // tile_side
    col_tiles = (nodes + halo_pad) // tile_side
    my_tiles = tiles[0, 0]
    slot_live = (jnp.arange(slots, dtype=jnp.int32) < tile_live[0, 0]).astype(jnp.float32)
    onehot = (tile_row[0, 0][:, None] == jnp.arange(row_tiles, dtype=jnp.int32)[None, :]).astype(
        jnp.float32
    )
    onehot = onehot * slot_live[:, None]
    pad_rows = jnp.zeros((halo_pad - owners * halo_width, width), jnp.bfloat16)
    current = features
    for step in range(HOPS):
        outgoing = current[send_index[0]]
        incoming = lax.all_to_all(outgoing, "rows", split_axis=0, concat_axis=0, tiled=True)
        extended = jnp.concatenate(
            [current, incoming.reshape(owners * halo_width, width), pad_rows], axis=0
        )
        picked = extended.reshape(col_tiles, tile_side, width)[tile_col[0, 0]]
        products = jnp.einsum("tij,tjf->tif", my_tiles, picked, preferred_element_type=jnp.float32)
        partial_value = jnp.einsum("tr,tif->rif", onehot, products).reshape(nodes, width)
        gathered = lax.psum(partial_value, "rep")
        current = update_rows(current, gathered, gain[step], w_in[step], w_out[step])
    return current


def solution(mesh):
    placed = (
        P("rows", None),
        P("rows", "rep", None, None, None),
        P("rows", "rep", None),
        P("rows", "rep", None),
        P("rows", "rep"),
        P("rows", None, None),
        P(),
        P(),
        P(),
    )
    return jax.shard_map(
        per_device, mesh=mesh, in_specs=placed, out_specs=P("rows", None), check_vma=False
    )
```

profile of v0, /device:TPU:8, one launch (start us, length us, event | category | flops | bytes accessed | tf_op | source)
XLA Modules:
  0.0 304.5 jit_solution(10579522859335403321)
XLA Ops:
  6.5 0.7 compare_select_fusion
  7.3 0.1 copy.12
  7.4 0.1 reshape.124
  7.5 2.5 gather_fusion
  10.1 0.8 reshape.123
  10.8 19.6 %all-to-all-start = ((bf16[128,4,256]{2,1,0:T(4,128)(2,1)}), bf16[128,4,256]{2,1,0:T(4,128)(2,1)S(1)}, u32[]{:S(2)}, u32[]{:S(2)}) async-start(bf16[128,4,256]{2,1,0:T(4,128)(2,1)} %reshape.123), calls=%async_computation | async-start | bytes 524288 | tf_op jit(solution)/shard_map/all_to_all | solution.py:39
  30.4 0.0 all-reduce.4.cloned.1.call-start
  31.2 0.6 copy-done.8
  31.8 21.4 %all-to-all-done = bf16[128,4,256]{2,1,0:T(4,128)(2,1)S(1)} async-done(((bf16[128,4,256]{2,1,0:T(4,128)(2,1)}), bf16[128,4,256]{2,1,0:T(4,128)(2,1)S(1)}, u32[]{:S(2)}, u32[]{:S(2)}) %all-to-all-start) | async-done | bytes 262176 | tf_op jit(solution)/shard_map/all_to_all | solution.py:39
  53.2 0.1 reshape.113
  53.3 0.6 gather_fusion.1
  53.9 0.3 fusion.58
  54.2 0.2 copy.16
  54.4 0.6 copy-done.9
  55.0 0.4 fusion.31
  55.5 0.8 copy.13
  56.3 0.0 all-reduce.4.cloned.1.call-update
  56.3 0.0 all-reduce.6.cloned.1.call-start
  56.4 0.6 copy-done.5
  57.0 49.1 %all-reduce.4.cloned.1.call-done = f32[512,256]{1,0:T(8,128)} async-done(((f32[512,256]{1,0:T(8,128)}), f32[512,256]{1,0:T(8,128)}) %all-reduce.4.cloned.1.call-update) | async-done | bytes 524304 | tf_op jit(solution)/shard_map/psum | solution.py:46
  106.1 1.3 multiply_reduce_fusion.2
  107.4 0.7 fusion
  108.1 2.0 gather_fusion.2
  110.0 0.1 reshape.139
  110.1 39.2 %all_to_all.15 = bf16[128,4,256]{2,1,0:T(4,128)(2,1)S(1)} all-to-all(bf16[128,4,256]{2,1,0:T(4,128)(2,1)S(1)} %reshape.139), channel_id=1, replica_groups=mesh['rep'=4,'rows'=128] {'rows'}, dimensions={0} | all-to-all | bytes 524288 | tf_op jit(solution)/shard_map/all_to_all | solution.py:39
  149.2 0.1 reshape.116
  149.4 0.6 gather_fusion.3
  149.9 0.3 fusion.56
  150.2 0.2 copy.17
  150.4 0.4 fusion.29
  150.8 0.8 copy.14
  151.7 0.0 all-reduce.6.cloned.1.call-update
  151.7 0.0 all-reduce.8.cloned.1.call-start
  151.7 49.0 %all-reduce.6.cloned.1.call-done = f32[512,256]{1,0:T(8,128)} async-done(((f32[512,256]{1,0:T(8,128)}), f32[512,256]{1,0:T(8,128)}) %all-reduce.6.cloned.1.call-update) | async-done | bytes 524304 | tf_op jit(solution)/shard_map/psum | solution.py:46
  200.7 1.3 multiply_reduce_fusion.1
  202.0 0.7 fusion.1
  202.7 2.0 gather_fusion.4
  204.6 0.1 reshape.155
  204.7 39.2 %all_to_all.16 = bf16[128,4,256]{2,1,0:T(4,128)(2,1)S(1)} all-to-all(bf16[128,4,256]{2,1,0:T(4,128)(2,1)S(1)} %reshape.155), channel_id=1, replica_groups=mesh['rep'=4,'rows'=128] {'rows'}, dimensions={0} | all-to-all | bytes 524288 | tf_op jit(solution)/shard_map/all_to_all | solution.py:39
  243.9 0.1 reshape.119
  244.0 0.6 gather_fusion.5
  244.6 0.3 fusion.54
  244.8 0.2 copy.18
  245.0 0.4 fusion.27
  245.4 0.8 copy.15
  246.3 49.0 %all-reduce.8.cloned.1.call-done = f32[512,256]{1,0:T(8,128)} async-done(((f32[512,256]{1,0:T(8,128)}), f32[512,256]{1,0:T(8,128)}) %all-reduce.8.cloned.1.call-update) | async-done | bytes 524304 | tf_op jit(solution)/shard_map/psum | solution.py:46
  295.3 1.3 multiply_reduce_fusion
  296.6 1.4 fusion.2
  (29 shorter events, 0.2 us)
Async XLA Ops:
  6.5 47.3 %copy-start = (bf16[1,1,2,256,256]{4,3,2,1,0:T(8,128)(2,1)S(1)}, bf16[1,1,2,256,256]{4,3,2,1,0:T(8,128)(2,1)}, u32[]{:S(2)}) copy-start(bf16[1,1,2,256,256]{4,3,2,1,0:T(8,128)(2,1)} %param.10) | copy-start | bytes 786436
  10.8 42.4 %all-to-all-start = ((bf16[128,4,256]{2,1,0:T(4,128)(2,1)}), bf16[128,4,256]{2,1,0:T(4,128)(2,1)S(1)}, u32[]{:S(2)}, u32[]{:S(2)}) async-start(bf16[128,4,256]{2,1,0:T(4,128)(2,1)} %reshape.123), calls=%async_computation | async-start | bytes 524288 | tf_op jit(solution)/shard_map/all_to_all | solution.py:39
  30.4 75.6 %all-reduce.4.cloned.1.call-start = ((), (), s32[]{:S(2)}) async-start(), calls=%async_computation.3 | async-start | bytes 1048576 | tf_op jit(solution)/shard_map/psum | solution.py:46
  31.1 0.7 copy-start.8
  31.8 21.4 %copy-start.1 = (bf16[512,256]{1,0:T(8,128)(2,1)S(1)}, bf16[512,256]{1,0:T(8,128)(2,1)}, u32[]{:S(2)}) copy-start(bf16[512,256]{1,0:T(8,128)(2,1)} %param.9) | copy-start | bytes 786436
  54.4 0.7 copy-start.9
  55.4 51.9 %copy-start.6 = (bf16[3,512,256]{2,1,0:T(8,128)(2,1)S(1)}, bf16[3,512,256]{2,1,0:T(8,128)(2,1)}, u32[]{:S(2)}) copy-start(bf16[3,512,256]{2,1,0:T(8,128)(2,1)} %param.17) | copy-start | bytes 2359300
  55.4 51.9 %copy-start.7 = (bf16[3,256,512]{2,1,0:T(8,128)(2,1)S(1)}, bf16[3,256,512]{2,1,0:T(8,128)(2,1)}, u32[]{:S(2)}) copy-start(bf16[3,256,512]{2,1,0:T(8,128)(2,1)} %param.16) | copy-start | bytes 2359300
  56.3 0.7 copy-start.5
  56.3 144.4 %all-reduce.6.cloned.1.call-start = ((), (), s32[]{:S(2)}) async-start(), calls=%async_computation.4 | async-start | bytes 1048576 | tf_op jit(solution)/shard_map/psum | solution.py:46
  106.1 1.3 copy-start.2
  151.7 143.6 %all-reduce.8.cloned.1.call-start = ((), (), s32[]{:S(2)}) async-start(), calls=%async_computation.5 | async-start | bytes 1048576 | tf_op jit(solution)/shard_map/psum | solution.py:46
  200.7 1.3 copy-start.3
  295.3 1.3 copy-start.4
Sparse Core Ops, SparseCore 0:
  56.4 49.5 all-reduce.3
  151.8 48.8 all-reduce.5
  246.4 48.8 all-reduce.7
where the time goes:
time: 305 us; the launch traced here: 304 us
  waiting for transfers between devices  168 us (55%)
  blocking collectives  78.3 us (26%)
  starting transfers between devices  19.7 us (6%)
  local copies, waits for them, and re-layouts  14.5 us (5%)
  between operations  14.1 us (5%)
  matrix products  4.75 us (2%)
  other arithmetic  4.68 us (2%)
    psum x3, waiting for transfers between devices, per_device(): gathered = lax.psum(partial_value, 'rep')  147 us
    all_to_all x2, blocking collectives, per_device(): lax.all_to_all(outgoing, 'rows', split_axis=0, concat_axis=0, tiled=True)  78.3 us
    all_to_all x1, waiting for transfers between devices, per_device(): lax.all_to_all(outgoing, 'rows', split_axis=0, concat_axis=0, tiled=True)  21.4 us
    all_to_all x1, starting transfers between devices, per_device(): lax.all_to_all(outgoing, 'rows', split_axis=0, concat_axis=0, tiled=True)  19.6 us
    gather x6, local copies, waits for them, and re-layouts, per_device(): outgoing = current[send_index[0]]  7.36 us
  transfers between devices with their start and end apart: 4, of which 4 were waited for; matrix products, arithmetic and copies ran while one was open for 0% of the time, Pallas kernels for 0%

commit v1 on v0

--- a/solution.py
+++ b/solution.py
@@ -43,7 +43,7 @@
         picked = extended.reshape(col_tiles, tile_side, width)[tile_col[0, 0]]
         products = jnp.einsum("tij,tjf->tif", my_tiles, picked, preferred_element_type=jnp.float32)
         partial_value = jnp.einsum("tr,tif->rif", onehot, products).reshape(nodes, width)
-        gathered = lax.psum(partial_value, "rep")
+        gathered = jnp.sum(lax.all_gather(partial_value, "rep"), axis=0)
         current = update_rows(current, gathered, gain[step], w_in[step], w_out[step])
     return current
 

time: 305 us -> 246 us (0.81)
  the two profiles are of different devices: /device:TPU:8 before, /device:TPU:1 now
where the time goes in v1:
time: 246 us
  waiting for transfers between devices  109 us (44%)
  blocking collectives  78 us (32%)
  starting transfers between devices  20.8 us (8%)
  between operations  14 us (6%)
  local copies, waits for them, and re-layouts  12.5 us (5%)
  other arithmetic  6.78 us (3%)
  matrix products  4.77 us (2%)
    all_gather x3, waiting for transfers between devices, per_device(): gathered = jnp.sum(lax.all_gather(partial_value, 'rep'), axis=0)  86.9 us
    all_to_all x2, blocking collectives, per_device(): lax.all_to_all(outgoing, 'rows', split_axis=0, concat_axis=0, tiled=True)  78 us
    all_to_all x1, waiting for transfers between devices, per_device(): lax.all_to_all(outgoing, 'rows', split_axis=0, concat_axis=0, tiled=True)  21.6 us
    all_to_all x1, starting transfers between devices, per_device(): lax.all_to_all(outgoing, 'rows', split_axis=0, concat_axis=0, tiled=True)  20.7 us
    gather x6, local copies, waits for them, and re-layouts, per_device(): outgoing = current[send_index[0]]  7.36 us
    reduce_sum x3, other arithmetic, per_device(): gathered = jnp.sum(lax.all_gather(partial_value, 'rep'), axis=0)  5.42 us
  transfers between devices with their start and end apart: 4, of which 4 were waited for; matrix products, arithmetic and copies ran while one was open for 0% of the time, Pallas kernels for 0%

profile of v1, /device:TPU:1, one launch (start us, length us, event | category | flops | bytes accessed | tf_op | source)
XLA Modules:
  0.0 245.6 jit_solution(14576182658137599172)
XLA Ops:
  6.5 0.8 compare_select_fusion
  7.3 0.1 copy.21
  7.4 0.1 reshape.112
  7.5 2.5 %gather_fusion = bf16[512,256]{1,0:T(8,128)(2,1)S(1)} fusion(bf16[512,256]{1,0:T(8,128)(2,1)} %param.9, s32[1024]{0:T(1024)S(1)} %pad_clamp_fusion.1), kind=kCustom, calls=%fused_computation | custom fusion | bytes 526336 | tf_op jit(solution)/shard_map/gather | solution.py:38
  10.1 0.8 reshape.111
  10.9 20.7 %all-to-all-start = ((bf16[128,4,256]{2,1,0:T(4,128)(2,1)}), bf16[128,4,256]{2,1,0:T(4,128)(2,1)S(1)}, u32[]{:S(2)}, u32[]{:S(2)}) async-start(bf16[128,4,256]{2,1,0:T(4,128)(2,1)} %reshape.111), calls=%async_computation | async-start | bytes 524288 | tf_op jit(solution)/shard_map/all_to_all | solution.py:39
  31.5 0.0 all-gather.4.cloned.1.call-start
  32.3 21.6 %all-to-all-done = bf16[128,4,256]{2,1,0:T(4,128)(2,1)S(1)} async-done(((bf16[128,4,256]{2,1,0:T(4,128)(2,1)}), bf16[128,4,256]{2,1,0:T(4,128)(2,1)S(1)}, u32[]{:S(2)}, u32[]{:S(2)}) %all-to-all-start) | async-done | bytes 262176 | tf_op jit(solution)/shard_map/all_to_all | solution.py:39
  53.9 0.1 reshape.104
  54.1 0.6 gather_fusion.1
  54.7 0.3 convolution_bitcast_fusion.2
  54.9 0.2 copy.23
  55.1 0.4 fusion.78
  55.6 0.8 copy.24
  56.4 0.0 all-gather.4.cloned.1.call-update
  56.4 0.0 all-gather.6.cloned.1.call-start
  56.5 29.8 %all-gather.4.cloned.1.call-done = f32[4,512,256]{2,1,0:T(8,128)} async-done(((f32[1,512,256]{2,1,0:T(8,128)}), f32[4,512,256]{2,1,0:T(8,128)}) %all-gather.4.cloned.1.call-update) | async-done | bytes 2097168 | tf_op jit(solution)/shard_map/all_gather | solution.py:46
  86.3 1.8 reduce_sum.54
  88.1 0.1 multiply_reduce_fusion.2
  88.3 0.7 fusion
  88.9 2.0 gather_fusion.2
  90.9 0.1 reshape.127
  91.0 39.0 %all_to_all.15 = bf16[128,4,256]{2,1,0:T(4,128)(2,1)S(1)} all-to-all(bf16[128,4,256]{2,1,0:T(4,128)(2,1)S(1)} %reshape.127), channel_id=1, replica_groups=mesh['rep'=4,'rows'=128] {'rows'}, dimensions={0} | all-to-all | bytes 524288 | tf_op jit(solution)/shard_map/all_to_all | solution.py:39
  130.0 0.1 reshape.106
  130.1 0.6 gather_fusion.3
  130.7 0.3 convolution_bitcast_fusion.1
  130.9 0.2 copy.26
  131.1 0.4 fusion.76
  131.6 0.8 copy.27
  132.4 0.0 all-gather.6.cloned.1.call-update
  132.4 0.0 all-gather.8.cloned.1.call-start
  132.5 28.5 %all-gather.6.cloned.1.call-done = f32[4,512,256]{2,1,0:T(8,128)} async-done(((f32[1,512,256]{2,1,0:T(8,128)}), f32[4,512,256]{2,1,0:T(8,128)}) %all-gather.6.cloned.1.call-update) | async-done | bytes 2097168 | tf_op jit(solution)/shard_map/all_gather | solution.py:46
  161.0 1.8 reduce_sum.56
  162.8 0.1 multiply_reduce_fusion.1
  163.0 0.7 fusion.1
  163.6 2.0 gather_fusion.4
  165.6 0.1 reshape.143
  165.7 39.0 %all_to_all.16 = bf16[128,4,256]{2,1,0:T(4,128)(2,1)S(1)} all-to-all(bf16[128,4,256]{2,1,0:T(4,128)(2,1)S(1)} %reshape.143), channel_id=1, replica_groups=mesh['rep'=4,'rows'=128] {'rows'}, dimensions={0} | all-to-all | bytes 524288 | tf_op jit(solution)/shard_map/all_to_all | solution.py:39
  204.7 0.1 reshape.108
  204.8 0.6 gather_fusion.5
  205.4 0.3 convolution_bitcast_fusion
  205.6 0.2 copy.29
  205.8 0.4 fusion.74
  206.3 0.8 copy.30
  207.1 28.6 %all-gather.8.cloned.1.call-done = f32[4,512,256]{2,1,0:T(8,128)} async-done(((f32[1,512,256]{2,1,0:T(8,128)}), f32[4,512,256]{2,1,0:T(8,128)}) %all-gather.8.cloned.1.call-update) | async-done | bytes 2097168 | tf_op jit(solution)/shard_map/all_gather | solution.py:46
  235.7 1.8 reduce_sum.58
  237.5 0.1 multiply_reduce_fusion
  237.7 1.4 fusion.2
  (26 shorter events, 0.2 us)
Async XLA Ops:
  6.5 48.1 %copy-start = (bf16[1,1,2,256,256]{4,3,2,1,0:T(8,128)(2,1)S(1)}, bf16[1,1,2,256,256]{4,3,2,1,0:T(8,128)(2,1)}, u32[]{:S(2)}) copy-start(bf16[1,1,2,256,256]{4,3,2,1,0:T(8,128)(2,1)} %param.10) | copy-start | bytes 786436
  6.5 47.5 %copy-start.1 = (bf16[512,256]{1,0:T(8,128)(2,1)S(1)}, bf16[512,256]{1,0:T(8,128)(2,1)}, u32[]{:S(2)}) copy-start(bf16[512,256]{1,0:T(8,128)(2,1)} %param.9) | copy-start | bytes 786436
  6.5 25.7 %copy-start.5 = (s32[1,1,2]{2,1,0:T(1,128)S(1)}, s32[1,1,2]{2,1,0:T(1,128)}, u32[]{:S(2)}) copy-start(s32[1,1,2]{2,1,0:T(1,128)} %param.12) | copy-start | bytes 28
  10.9 44.3 %copy-start.6 = (s32[1,1,2]{2,1,0:T(1,128)S(1)}, s32[1,1,2]{2,1,0:T(1,128)}, u32[]{:S(2)}) copy-start(s32[1,1,2]{2,1,0:T(1,128)} %param.11) | copy-start | bytes 28
  10.9 43.1 %all-to-all-start = ((bf16[128,4,256]{2,1,0:T(4,128)(2,1)}), bf16[128,4,256]{2,1,0:T(4,128)(2,1)S(1)}, u32[]{:S(2)}, u32[]{:S(2)}) async-start(bf16[128,4,256]{2,1,0:T(4,128)(2,1)} %reshape.111), calls=%async_computation | async-start | bytes 524288 | tf_op jit(solution)/shard_map/all_to_all | solution.py:39
  31.5 54.7 %all-gather.4.cloned.1.call-start = ((), (), s32[]{:S(2)}) async-start(), calls=%async_computation.3 | async-start | bytes 2621440 | tf_op jit(solution)/shard_map/all_gather | solution.py:46
  54.1 2.4 copy-start.2
  56.4 31.9 %copy-start.3 = (bf16[3,512,256]{2,1,0:T(8,128)(2,1)S(1)}, bf16[3,512,256]{2,1,0:T(8,128)(2,1)}, u32[]{:S(2)}) copy-start(bf16[3,512,256]{2,1,0:T(8,128)(2,1)} %param.17) | copy-start | bytes 2359300
  56.4 31.9 %copy-start.4 = (bf16[3,256,512]{2,1,0:T(8,128)(2,1)S(1)}, bf16[3,256,512]{2,1,0:T(8,128)(2,1)}, u32[]{:S(2)}) copy-start(bf16[3,256,512]{2,1,0:T(8,128)(2,1)} %param.16) | copy-start | bytes 2359300
  56.4 104.6 %all-gather.6.cloned.1.call-start = ((), (), s32[]{:S(2)}) async-start(), calls=%async_computation.4 | async-start | bytes 2621440 | tf_op jit(solution)/shard_map/all_gather | solution.py:46
  132.4 103.3 %all-gather.8.cloned.1.call-start = ((), (), s32[]{:S(2)}) async-start(), calls=%async_computation.5 | async-start | bytes 2621440 | tf_op jit(solution)/shard_map/all_gather | solution.py:46
Sparse Core Ops, SparseCore 0:
  56.5 29.6 all-gather.3
  132.5 28.4 all-gather.5
  207.2 28.4 all-gather.7
